TPU v7x, 512 devices: a whole 4x8x8 slice. The times are simulated.
512 devices in a mesh: row: 64 (over x, z, core), blk: 8 (over y).
Axes of the slice: x: 4, y: 8, z: 8, core: 2. Of those that a mesh axis runs over, the one named last changes fastest.
Arguments:
- factor_panel: bfloat16 [131072, 2, 2048], P('row', None, 'blk'), may hold values from -0.09375 to 0.09375
- right_side: float32 [256, 131072], P('blk', 'row'), may hold values from -6 to 6
- block_inverse: float32 [2, 2048, 2048], P(None, 'row', 'blk'), may hold values from -2 to 2, as said below
Outputs:
- solved: float32 [2, 256, 2048], P(None, 'blk', 'row')
- reduced_side: float32 [256, 131072], P('blk', 'row')
Inputs may be any that keep to these rules, and one draw needn't show every extreme that they name: block_inverse[k] is lower triangular with diagonal entries between 1 and 2.
All inputs are finite; a program needn't handle non-finite values.
Results may differ from a plain program's by a relative error of at most 0.015.
Values may be sent and summed in bfloat16 or wider, within the bound.
No kernel may reach another device: no remote copies, remote signals or barrier semaphores. Data moves between devices by JAX's collectives and lax.ppermute only.
A program may use at most 64 MiB of HBM per device.

v0:
```python
import jax
import jax.numpy as jnp
from jax import lax
from jax.sharding import PartitionSpec as P

STEPS = 2


def from_root(array, axis, root):
    mine = lax.axis_index(axis) == root
    return lax.psum(jnp.where(mine, array, jnp.zeros_like(array)), axis)


def local(factor_panel, right_side, block_inverse):
    blk_index = lax.axis_index("blk")
    row_index = lax.axis_index("row")
    dates_local = right_side.shape[0]
    width = factor_panel.shape[2]
    reduced_side = right_side
    outputs = []
    for section in range(STEPS):
        pivot_block = from_root(reduced_side, "row", section)
        pivot_cols = lax.all_to_all(pivot_block, "blk", split_axis=1, concat_axis=0, tiled=True)
        partial_value = jnp.dot(
            pivot_cols, block_inverse[section].T, precision=lax.Precision.HIGHEST
        )
        summed = lax.psum(partial_value, "blk")
        own_share = lax.dynamic_slice_in_dim(summed, blk_index * dates_local, dates_local, 0)
        gathered = lax.all_gather(summed.astype(jnp.bfloat16), "row", axis=1, tiled=True)
        group_cols = lax.dynamic_slice_in_dim(gathered, blk_index * width, width, 1)
        outputs.append(own_share)
        panel_now = factor_panel[:, section, :]
        update = lax.psum_scatter(
            lax.dot_general(
                group_cols, panel_now, (((1,), (1,)), ((), ())), preferred_element_type=jnp.float32
            ).astype(jnp.bfloat16),
            "blk",
            scatter_dimension=0,
            tiled=True,
        ).astype(jnp.float32)
        reduced_side = reduced_side - jnp.where(row_index > section, update, jnp.float32(0.0))
    return (jnp.stack(outputs), reduced_side)


def solution(mesh):
    placed = (P("row", None, "blk"), P("blk", "row"), P(None, "row", "blk"))
    return jax.shard_map(
        local,
        mesh=mesh,
        in_specs=placed,
        out_specs=(P(None, "blk", "row"), P("blk", "row")),
        check_vma=False,
    )
```

profile of v0, /device:TPU:4, one launch (start us, length us, event | category | flops | bytes accessed | tf_op | source)
XLA Modules:
  0.0 736.3 jit_solution(8217188928372666133)
XLA Ops:
  7.2 0.0 copy-start
  7.2 0.0 all-reduce.3.cloned.1.call-start
  7.3 0.7 copy.22
  8.0 0.0 all-reduce.3.cloned.1.call-update
  8.0 0.0 all-gather.3.cloned.1.call-start
  8.1 195.5 %all-reduce.3.cloned.1.call-done = f32[32,8,256]{2,0,1:T(8,128)} async-done(((f32[32,8,256]{2,0,1:T(8,128)}), f32[32,8,256]{2,0,1:T(8,128)}) %all-reduce.3.cloned.1.call-update) | async-done | bytes 262160 | tf_op jit(solution)/shard_map/psum | solution.py:11
  203.5 20.0 %all_to_all.38 = f32[32,8,256]{2,0,1:T(8,128)S(1)} all-to-all(f32[32,8,256]{2,0,1:T(8,128)} %all-reduce.3.cloned.1.call-done), channel_id=1, replica_groups=mesh['row'=64,'blk'=8] {'blk'}, dimensions={1} | all-to-all | bytes 524288 | tf_op jit(solution)/shard_map/all_to_all | solution.py:23
  223.5 1.1 fusion.5
  224.6 27.3 %psum.29 = f32[256,32]{0,1:T(8,128)S(1)} all-reduce(f32[256,32]{0,1:T(8,128)S(1)} %fusion.5), channel_id=1, replica_groups=mesh['row'=64,'blk'=8] {'blk'}, use_global_device_ids=true, to_apply=%region_1.2 | all-reduce | flops 8192 | bytes 65536 | tf_op jit(solution)/shard_map/psum | solution.py:27
  251.9 0.6 convert_element_type.18
  252.5 0.0 all-gather.3.cloned.1.call-update
  252.6 0.0 reduce-scatter.3.cloned.1.call-start
  252.6 0.0 copy-done
  252.6 4.2 fusion.11
  256.8 0.0 copy-start.2
  256.8 71.7 %all-gather.3.cloned.1.call-done = bf16[256,2048]{0,1:T(8,128)(2,1)} async-done(((bf16[256,32]{0,1:T(8,128)(2,1)}), bf16[256,2048]{0,1:T(8,128)(2,1)}) %all-gather.3.cloned.1.call-update) | async-done | bytes 1048592 | tf_op jit(solution)/shard_map/all_gather | solution.py:29
  328.6 0.0 copy-start.4
  328.6 3.2 convolution_convert_fusion.1
  331.7 0.0 copy-start.1
  331.8 0.0 reduce-scatter.3.cloned.1.call-update
  331.8 0.0 all-reduce.5.cloned.1.call-start
  331.8 39.6 %reduce-scatter.3.cloned.1.call-done = bf16[32,2048]{1,0:T(8,128)(2,1)} async-done(((bf16[256,2048]{1,0:T(8,128)(2,1)}), bf16[32,2048]{1,0:T(8,128)(2,1)}) %reduce-scatter.3.cloned.1.call-update) | async-done | bytes 131088 | tf_op jit(solution)/shard_map/reduce_scatter | solution.py:33
  371.4 0.0 copy-done.2
  371.4 0.9 fusion
  372.4 0.7 copy.21
  373.1 0.0 all-reduce.5.cloned.1.call-update
  373.1 0.0 all-gather.5.cloned.1.call-start
  373.2 188.1 %all-reduce.5.cloned.1.call-done = f32[32,8,256]{2,0,1:T(8,128)} async-done(((f32[32,8,256]{2,0,1:T(8,128)}), f32[32,8,256]{2,0,1:T(8,128)}) %all-reduce.5.cloned.1.call-update) | async-done | bytes 262160 | tf_op jit(solution)/shard_map/psum | solution.py:11
  561.3 20.0 %all_to_all.39 = f32[32,8,256]{2,0,1:T(8,128)S(1)} all-to-all(f32[32,8,256]{2,0,1:T(8,128)} %all-reduce.5.cloned.1.call-done), channel_id=1, replica_groups=mesh['row'=64,'blk'=8] {'blk'}, dimensions={1} | all-to-all | bytes 524288 | tf_op jit(solution)/shard_map/all_to_all | solution.py:23
  581.3 0.0 copy-start.3
  581.3 0.0 copy-done.4
  581.3 0.3 fusion.3
  581.6 27.3 %psum.31 = f32[256,32]{0,1:T(8,128)S(1)} all-reduce(f32[256,32]{0,1:T(8,128)S(1)} %fusion.3), channel_id=1, replica_groups=mesh['row'=64,'blk'=8] {'blk'}, use_global_device_ids=true, to_apply=%region_4.5 | all-reduce | flops 8192 | bytes 65536 | tf_op jit(solution)/shard_map/psum | solution.py:27
  608.9 0.6 convert_element_type.21
  609.5 0.0 all-gather.5.cloned.1.call-update
  609.6 0.0 reduce-scatter.5.cloned.1.call-start
  609.6 75.9 %all-gather.5.cloned.1.call-done = bf16[256,2048]{0,1:T(8,128)(2,1)} async-done(((bf16[256,32]{0,1:T(8,128)(2,1)}), bf16[256,2048]{0,1:T(8,128)(2,1)}) %all-gather.5.cloned.1.call-update) | async-done | bytes 1048592 | tf_op jit(solution)/shard_map/all_gather | solution.py:29
  685.6 0.0 copy-done.1
  685.6 2.4 convolution_convert_fusion
  687.9 0.0 reduce-scatter.5.cloned.1.call-update
  688.0 0.1 constant_dynamic-slice_fusion.1
  688.0 0.1 copy.6
  688.1 0.1 constant_dynamic-slice_fusion
  688.2 0.1 copy.9
  688.3 0.6 pad_maximum_fusion
  688.9 38.9 %reduce-scatter.5.cloned.1.call-done = bf16[32,2048]{1,0:T(8,128)(2,1)} async-done(((bf16[256,2048]{1,0:T(8,128)(2,1)}), bf16[32,2048]{1,0:T(8,128)(2,1)}) %reduce-scatter.5.cloned.1.call-update) | async-done | bytes 131088 | tf_op jit(solution)/shard_map/reduce_scatter | solution.py:33
  727.7 0.0 copy-done.3
  727.7 1.7 select_subtract_fusion
  (1 shorter events, 0.0 us)
Async XLA Ops:
  7.2 245.5 %copy-start = (bf16[2048,2,256]{2,1,0:T(2,128)(2,1)S(1)}, bf16[2048,2,256]{2,1,0:T(2,128)(2,1)}, u32[]{:S(2)}) copy-start(bf16[2048,2,256]{2,1,0:T(2,128)(2,1)} %param.3) | copy-start | bytes 6291460
  7.2 196.4 %all-reduce.3.cloned.1.call-start = ((), (), s32[]{:S(2)}) async-start(), calls=%async_computation.4 | async-start | bytes 524288 | tf_op jit(solution)/shard_map/psum | solution.py:11
  8.0 320.5 %all-gather.3.cloned.1.call-start = ((), (), s32[]{:S(2)}) async-start(), calls=%async_computation.5 | async-start | bytes 1064960 | tf_op jit(solution)/shard_map/all_gather | solution.py:29
  252.6 118.9 %reduce-scatter.3.cloned.1.call-start = ((), (), s32[]{:S(2)}) async-start(), calls=%async_computation.6 | async-start | bytes 1179648 | tf_op jit(solution)/shard_map/reduce_scatter | solution.py:33
  256.8 114.6 %copy-start.2 = (f32[32,2048]{1,0:T(8,128)S(1)}, f32[32,2048]{1,0:T(8,128)}, u32[]{:S(2)}) copy-start(f32[32,2048]{1,0:T(8,128)} %param.4) | copy-start | bytes 786436
  328.6 252.7 %copy-start.4 = (f32[2,32,256]{2,1,0:T(8,128)S(1)}, f32[2,32,256]{2,1,0:T(8,128)}, u32[]{:S(2)}) copy-start(f32[2,32,256]{2,1,0:T(8,128)} %param.5) | copy-start | bytes 196612
  331.7 353.8 %copy-start.1 = (bf16[2048,1,256]{2,1,0:T(2,128)(2,1)S(1)}, bf16[2048,1,256]{2,1,0:T(2,128)(2,1)}, u32[]{:S(2)}) copy-start(bf16[2048,1,256]{2,1,0:T(2,128)(2,1)} %get-tuple-element.2) | copy-start | bytes 3145732
  331.8 229.5 %all-reduce.5.cloned.1.call-start = ((), (), s32[]{:S(2)}) async-start(), calls=%async_computation.7 | async-start | bytes 524288 | tf_op jit(solution)/shard_map/psum | solution.py:11
  373.1 312.4 %all-gather.5.cloned.1.call-start = ((), (), s32[]{:S(2)}) async-start(), calls=%async_computation.8 | async-start | bytes 1064960 | tf_op jit(solution)/shard_map/all_gather | solution.py:29
  581.3 146.5 %copy-start.3 = (bf16[32,2048]{1,0:T(8,128)(2,1)S(1)}, bf16[32,2048]{1,0:T(8,128)(2,1)}, u32[]{:S(2)}) copy-start(bf16[32,2048]{1,0:T(8,128)(2,1)} %reduce-scatter.3.cloned.1.call-done) | copy-start | bytes 393220
  609.6 118.2 %reduce-scatter.5.cloned.1.call-start = ((), (), s32[]{:S(2)}) async-start(), calls=%async_computation.9 | async-start | bytes 1179648 | tf_op jit(solution)/shard_map/reduce_scatter | solution.py:33
Sparse Core Ops, SparseCore 0:
  12.0 191.4 all-reduce.2
  252.7 75.8 all-gather.2
  331.9 39.4 reduce-scatter.2
  375.3 185.9 all-reduce.4
  609.7 75.8 all-gather.4
  688.2 39.4 reduce-scatter.4
where the time goes:
time: 737 us; the launch traced here: 736 us
  waiting for transfers between devices  610 us (83%)
  blocking collectives  94.6 us (13%)
  between operations  14.2 us (2%)
    psum x2, waiting for transfers between devices, from_root(): return lax.psum(jnp.where(mine, array, jnp.zeros_like(array)), axis)  384 us
    all_gather x2, waiting for transfers between devices, local(): lax.all_gather(summed.astype(jnp.bfloat16), 'row', axis=1, tiled=True)  148 us
    reduce_scatter x2, waiting for transfers between devices, local(): lax.psum_scatter(lax.dot_general(group_cols, panel_now, (((1,), (1,)), ((...  78.4 us
    psum x2, blocking collectives, local(): summed = lax.psum(partial_value, 'blk')  54.6 us
    all_to_all x2, blocking collectives, local(): lax.all_to_all(pivot_block, 'blk', split_axis=1, concat_axis=0, tiled=True)  40 us
  transfers between devices with their start and end apart: 6, of which 6 were waited for; matrix products, arithmetic and copies ran while one was open for 1% of the time, Pallas kernels for 0%

commit v1 on v0

--- a/solution.py
+++ b/solution.py
@@ -26,7 +26,11 @@
         )
         summed = lax.psum(partial_value, "blk")
         own_share = lax.dynamic_slice_in_dim(summed, blk_index * dates_local, dates_local, 0)
-        gathered = lax.all_gather(summed.astype(jnp.bfloat16), "row", axis=1, tiled=True)
+        x = summed.astype(jnp.bfloat16)
+        count = lax.axis_size("row")
+        tiles = jnp.stack([x for _ in range(count)])
+        tiles = lax.all_to_all(tiles, "row", split_axis=0, concat_axis=0)
+        gathered = jnp.concatenate(tiles, axis=1)
         group_cols = lax.dynamic_slice_in_dim(gathered, blk_index * width, width, 1)
         outputs.append(own_share)
         panel_now = factor_panel[:, section, :]

time: 737 us -> 644 us (0.87)
  the two profiles are of different devices: /device:TPU:4 before, /device:TPU:2 now
where the time goes in v1:
time: 644 us; the launch traced here: 643 us
  waiting for transfers between devices  480 us (75%)
  blocking collectives  127 us (20%)
  between operations  13.9 us (2%)
  local copies, waits for them, and re-layouts  7.21 us (1%)
    psum x2, waiting for transfers between devices, from_root(): return lax.psum(jnp.where(mine, array, jnp.zeros_like(array)), axis)  385 us
    reduce_scatter x2, waiting for transfers between devices, local(): lax.psum_scatter(lax.dot_general(group_cols, panel_now, (((1,), (1,)), ((...  72.1 us
    psum x2, blocking collectives, local(): summed = lax.psum(partial_value, 'blk')  54.6 us
    all_to_all x2, blocking collectives, local(): lax.all_to_all(pivot_block, 'blk', split_axis=1, concat_axis=0, tiled=True)  40 us
    all_to_all x1, blocking collectives, local(): tiles = lax.all_to_all(tiles, 'row', split_axis=0, concat_axis=0)  32.4 us
    all_to_all x1, waiting for transfers between devices, local(): tiles = lax.all_to_all(tiles, 'row', split_axis=0, concat_axis=0)  22.7 us
  transfers between devices with their start and end apart: 5, of which 5 were waited for; matrix products, arithmetic and copies ran while one was open for 1% of the time, Pallas kernels for 0%

profile of v1, /device:TPU:2, one launch (start us, length us, event | category | flops | bytes accessed | tf_op | source)
XLA Modules:
  0.0 643.3 jit_solution(10224945748858545569)
XLA Ops:
  7.2 0.0 all-reduce.3.cloned.1.call-start
  7.3 0.7 copy.24
  8.0 0.0 all-reduce.3.cloned.1.call-update
  8.0 0.0 copy-start
  8.0 196.3 %all-reduce.3.cloned.1.call-done = f32[32,8,256]{2,0,1:T(8,128)} async-done(((f32[32,8,256]{2,0,1:T(8,128)}), f32[32,8,256]{2,0,1:T(8,128)}) %all-reduce.3.cloned.1.call-update) | async-done | bytes 262160 | tf_op jit(solution)/shard_map/psum | solution.py:11
  204.3 20.0 %all_to_all.48 = f32[32,8,256]{2,0,1:T(8,128)S(1)} all-to-all(f32[32,8,256]{2,0,1:T(8,128)} %all-reduce.3.cloned.1.call-done), channel_id=1, replica_groups=mesh['row'=64,'blk'=8] {'blk'}, dimensions={1} | all-to-all | bytes 524288 | tf_op jit(solution)/shard_map/all_to_all | solution.py:23
  224.3 1.1 fusion.5
  225.4 27.3 %psum.29 = f32[256,32]{0,1:T(8,128)S(1)} all-reduce(f32[256,32]{0,1:T(8,128)S(1)} %fusion.5), channel_id=1, replica_groups=mesh['row'=64,'blk'=8] {'blk'}, use_global_device_ids=true, to_apply=%region_1.2 | all-reduce | flops 8192 | bytes 65536 | tf_op jit(solution)/shard_map/psum | solution.py:27
  252.7 1.1 stack.11
  253.8 5.6 all-to-all-start.1
  259.4 0.0 reduce-scatter.3.cloned.1.call-start
  259.5 0.0 copy-done
  259.5 4.2 fusion.11
  263.7 0.0 copy-start.2
  263.7 22.7 %all-to-all-done.1 = bf16[64,256,32]{1,2,0:T(8,128)(2,1)S(1)} async-done(((bf16[64,256,32]{1,2,0:T(8,128)(2,1)}), bf16[64,256,32]{1,2,0:T(8,128)(2,1)S(1)}, u32[]{:S(2)}, u32[]{:S(2)}) %all-to-all-start.1) | async-done | bytes 1048608 | tf_op jit(solution)/shard_map/all_to_all | solution.py:32
  286.4 0.0 copy-start.4
  286.4 3.1 convolution_convert_fusion.1
  289.5 0.0 reduce-scatter.3.cloned.1.call-update
  289.5 0.0 all-reduce.5.cloned.1.call-start
  289.6 36.5 %reduce-scatter.3.cloned.1.call-done = bf16[32,2048]{1,0:T(8,128)(2,1)} async-done(((bf16[256,2048]{1,0:T(8,128)(2,1)}), bf16[32,2048]{1,0:T(8,128)(2,1)}) %reduce-scatter.3.cloned.1.call-update) | async-done | bytes 131088 | tf_op jit(solution)/shard_map/reduce_scatter | solution.py:37
  326.0 0.0 copy-done.2
  326.0 0.9 fusion
  327.0 0.7 copy.23
  327.7 0.0 all-reduce.5.cloned.1.call-update
  327.7 0.0 copy-start.1
  327.7 0.0 reduce-scatter.5.cloned.1.call-start
  327.8 189.1 %all-reduce.5.cloned.1.call-done = f32[32,8,256]{2,0,1:T(8,128)} async-done(((f32[32,8,256]{2,0,1:T(8,128)}), f32[32,8,256]{2,0,1:T(8,128)}) %all-reduce.5.cloned.1.call-update) | async-done | bytes 262160 | tf_op jit(solution)/shard_map/psum | solution.py:11
  516.9 20.0 %all_to_all.49 = f32[32,8,256]{2,0,1:T(8,128)S(1)} all-to-all(f32[32,8,256]{2,0,1:T(8,128)} %all-reduce.5.cloned.1.call-done), channel_id=1, replica_groups=mesh['row'=64,'blk'=8] {'blk'}, dimensions={1} | all-to-all | bytes 524288 | tf_op jit(solution)/shard_map/all_to_all | solution.py:23
  536.9 0.0 copy-done.4
  536.9 0.3 fusion.3
  537.2 27.3 %psum.31 = f32[256,32]{0,1:T(8,128)S(1)} all-reduce(f32[256,32]{0,1:T(8,128)S(1)} %fusion.3), channel_id=1, replica_groups=mesh['row'=64,'blk'=8] {'blk'}, use_global_device_ids=true, to_apply=%region_4.5 | all-reduce | flops 8192 | bytes 65536 | tf_op jit(solution)/shard_map/psum | solution.py:27
  564.5 0.1 stack.14
  564.7 32.4 %all_to_all.50 = bf16[64,256,32]{1,2,0:T(8,128)(2,1)S(1)} all-to-all(bf16[64,256,32]{1,2,0:T(8,128)(2,1)S(1)} %stack.14), channel_id=1, replica_groups=mesh['row'=64,'blk'=8] {'row'}, dimensions={0} | all-to-all | bytes 2097152 | tf_op jit(solution)/shard_map/all_to_all | solution.py:32
  597.0 0.0 copy-start.3
  597.0 0.0 copy-done.1
  597.0 1.5 convolution_convert_fusion
  598.5 0.0 reduce-scatter.5.cloned.1.call-update
  598.6 0.1 constant_dynamic-slice_fusion.1
  598.7 0.1 copy.8
  598.7 0.1 constant_dynamic-slice_fusion
  598.8 0.1 copy.11
  598.9 0.6 pad_maximum_fusion
  599.5 35.6 %reduce-scatter.5.cloned.1.call-done = bf16[32,2048]{1,0:T(8,128)(2,1)} async-done(((bf16[256,2048]{1,0:T(8,128)(2,1)}), bf16[32,2048]{1,0:T(8,128)(2,1)}) %reduce-scatter.5.cloned.1.call-update) | async-done | bytes 131088 | tf_op jit(solution)/shard_map/reduce_scatter | solution.py:37
  635.1 0.0 copy-done.3
  635.1 1.7 select_subtract_fusion
  (3 shorter events, 0.0 us)
Async XLA Ops:
  7.2 197.1 %all-reduce.3.cloned.1.call-start = ((), (), s32[]{:S(2)}) async-start(), calls=%async_computation.6 | async-start | bytes 524288 | tf_op jit(solution)/shard_map/psum | solution.py:11
  8.0 251.5 %copy-start = (bf16[2048,2,256]{2,1,0:T(2,128)(2,1)S(1)}, bf16[2048,2,256]{2,1,0:T(2,128)(2,1)}, u32[]{:S(2)}) copy-start(bf16[2048,2,256]{2,1,0:T(2,128)(2,1)} %param.3) | copy-start | bytes 6291460
  253.8 32.6 %all-to-all-start.1 = ((bf16[64,256,32]{1,2,0:T(8,128)(2,1)}), bf16[64,256,32]{1,2,0:T(8,128)(2,1)S(1)}, u32[]{:S(2)}, u32[]{:S(2)}) async-start(bf16[64,256,32]{1,2,0:T(8,128)(2,1)} %stack.11), calls=%async_computation.1 | async-start | bytes 2097152 | tf_op jit(solution)/shard_map/all_to_all | solution.py:32
  259.4 66.6 %reduce-scatter.3.cloned.1.call-start = ((), (), s32[]{:S(2)}) async-start(), calls=%async_computation.7 | async-start | bytes 1179648 | tf_op jit(solution)/shard_map/reduce_scatter | solution.py:37
  263.7 62.3 %copy-start.2 = (f32[32,2048]{1,0:T(8,128)S(1)}, f32[32,2048]{1,0:T(8,128)}, u32[]{:S(2)}) copy-start(f32[32,2048]{1,0:T(8,128)} %param.4) | copy-start | bytes 786436
  286.4 250.5 %copy-start.4 = (f32[2,32,256]{2,1,0:T(8,128)S(1)}, f32[2,32,256]{2,1,0:T(8,128)}, u32[]{:S(2)}) copy-start(f32[2,32,256]{2,1,0:T(8,128)} %param.5) | copy-start | bytes 196612
  289.5 227.4 %all-reduce.5.cloned.1.call-start = ((), (), s32[]{:S(2)}) async-start(), calls=%async_computation.8 | async-start | bytes 524288 | tf_op jit(solution)/shard_map/psum | solution.py:11
  327.7 269.3 %copy-start.1 = (bf16[2048,1,256]{2,1,0:T(2,128)(2,1)S(1)}, bf16[2048,1,256]{2,1,0:T(2,128)(2,1)}, u32[]{:S(2)}) copy-start(bf16[2048,1,256]{2,1,0:T(2,128)(2,1)} %get-tuple-element.2) | copy-start | bytes 3145732
  327.7 307.3 %reduce-scatter.5.cloned.1.call-start = ((), (), s32[]{:S(2)}) async-start(), calls=%async_computation.9 | async-start | bytes 1179648 | tf_op jit(solution)/shard_map/reduce_scatter | solution.py:37
  597.0 38.1 %copy-start.3 = (bf16[32,2048]{1,0:T(8,128)(2,1)S(1)}, bf16[32,2048]{1,0:T(8,128)(2,1)}, u32[]{:S(2)}) copy-start(bf16[32,2048]{1,0:T(8,128)(2,1)} %reduce-scatter.3.cloned.1.call-done) | copy-start | bytes 393220
Sparse Core Ops, SparseCore 0:
  12.0 192.2 all-reduce.2
  289.6 36.3 reduce-scatter.2
  330.1 186.7 all-reduce.4
  598.7 36.3 reduce-scatter.4
